TPU v7x, 32 devices: a whole 2x2x4 slice. The times are simulated.
32 devices in a mesh: grp: 2 (over y), seq: 4 (over z), wid: 2 (over x), rep: 2 (over core).
Axes of the slice: x: 2, y: 2, z: 4, core: 2. Of those that a mesh axis runs over, the one named last changes fastest.
Arguments:
- activations: bfloat16 [8192, 8192], P(('grp', 'seq'), ('wid', 'rep')), parts along dimension 0, may hold values from -6 to 6
- output_grads: bfloat16 [8192, 8192], P(('grp', 'seq'), ('wid', 'rep')), parts along dimension 0, may hold values from -6 to 6
- act_exponents: int32 [128, 64], P(('grp', 'seq'), ('wid', 'rep')), parts along dimension 0, may hold values from -2 to 2
- grad_exponents: int32 [128, 64], P(('grp', 'seq'), ('wid', 'rep')), parts along dimension 0, may hold values from -2 to 2
- input_blocks: bfloat16 [16, 128, 64], P(('wid', 'rep')), may hold values from -0.125 to 0.125
- input_index: int32 [16], P(('wid', 'rep')), may hold values from 0 to 63, as said below
- output_blocks: bfloat16 [16, 128, 64], P(('wid', 'rep')), may hold values from -0.125 to 0.125
- output_index: int32 [16], P(('wid', 'rep')), may hold values from 0 to 63, as said below
- fisher_inverse: float32 [4096, 4096], P('seq', 'wid'), may hold values from -1 to 7, as said below
Outputs:
- preconditioned: float32 [64, 2, 4096], P(('grp', 'wid'), 'rep', 'seq'), parts along dimension 0
There are 2 independent parts, one for each index of `grp`. A program takes and returns all parts, laid end to end along the dimension named above; an argument that names none is the same for every part. Nothing has to cross between parts.
Inputs may be any that keep to these rules, and one draw needn't show every extreme that they name: `input_index`: Rising; exactly one index in each aligned run of 4 blocks; the first block and the last block are always named. `output_index`: Rising; exactly one index in each aligned run of 4 blocks; the first block and the last block are always named. `fisher_inverse`: Symmetric.
All inputs are finite; a program needn't handle non-finite values.
Results may differ from a plain program's by a relative error of at most 0.00045.
Values sent between devices are 32-bit elements; how exact they have to be, the bound alone decides.
A program may use at most 64 MiB of HBM per device.

v0:
```python
import jax
import jax.numpy as jnp
from jax import lax
from jax.sharding import PartitionSpec as P

BLK = 128
LEN = 64


def select_blocks(values, exponents, index, wid_count, rep_count):
    tok_rows = values.shape[0]
    block_count = values.shape[1] // BLK
    seq_local = tok_rows // LEN
    per_device = seq_local // (wid_count * rep_count)
    local_index = index % block_count
    blocks = values.reshape(seq_local, LEN, block_count, BLK)
    picked = jnp.take(blocks, local_index, axis=2)
    scaling = jnp.exp2(jnp.take(exponents, local_index, axis=1).astype(jnp.float32)).astype(
        jnp.bfloat16
    )
    scaled = picked * scaling[:, None, :, None]
    width = index.shape[0] * BLK
    scaled = scaled.reshape(wid_count, per_device, rep_count, LEN, width)
    return jnp.transpose(scaled, (0, 2, 1, 3, 4)).reshape(tok_rows, width)


def tile_product(piece_rows, fisher_tile):
    return lax.dot_general(
        piece_rows,
        fisher_tile,
        (((1,), (1,)), ((), ())),
        precision=lax.Precision.HIGHEST,
        preferred_element_type=jnp.float32,
    )


def shards(
    activations,
    output_grads,
    act_exponents,
    grad_exponents,
    input_blocks,
    input_index,
    output_blocks,
    output_index,
    fisher_inverse,
):
    wid_count = lax.axis_size("wid")
    rep_count = lax.axis_size("rep")
    width_proj = input_blocks.shape[2]
    picked_acts = select_blocks(activations, act_exponents, input_index, wid_count, rep_count)
    picked_grads = select_blocks(output_grads, grad_exponents, output_index, wid_count, rep_count)
    input_flat = input_blocks.reshape(-1, width_proj)
    output_flat = output_blocks.reshape(-1, width_proj)
    act_part = jnp.dot(picked_acts, input_flat, preferred_element_type=jnp.float32)
    grad_part = jnp.dot(picked_grads, output_flat, preferred_element_type=jnp.float32)
    projected = lax.psum_scatter(
        jnp.concatenate([act_part, grad_part], axis=1),
        ("wid", "rep"),
        scatter_dimension=0,
        tiled=True,
    )
    per_device = projected.shape[0] // LEN
    act_proj = projected[:, :width_proj].reshape(per_device, LEN, width_proj)
    grad_proj = projected[:, width_proj:].reshape(per_device, LEN, width_proj)
    outer = jnp.einsum("lti,ltj->lij", grad_proj, act_proj, precision=lax.Precision.HIGHEST) / LEN
    flat = outer.reshape(per_device, width_proj * width_proj)
    routed = lax.all_to_all(flat, "wid", split_axis=1, concat_axis=0, tiled=True)
    partial_value = tile_product(lax.all_gather(routed, "seq", axis=0, tiled=True), fisher_inverse)
    result = lax.psum_scatter(partial_value, "wid", scatter_dimension=0, tiled=True)
    return result.reshape(result.shape[0], 1, result.shape[1])


def solution(mesh):
    placed = (
        P(("grp", "seq"), ("wid", "rep")),
        P(("grp", "seq"), ("wid", "rep")),
        P(("grp", "seq"), ("wid", "rep")),
        P(("grp", "seq"), ("wid", "rep")),
        P(("wid", "rep"), None, None),
        P(("wid", "rep")),
        P(("wid", "rep"), None, None),
        P(("wid", "rep")),
        P("seq", "wid"),
    )
    return jax.shard_map(
        shards,
        mesh=mesh,
        in_specs=placed,
        out_specs=P(("grp", "wid"), "rep", "seq"),
        check_vma=False,
    )
```

profile of v0, /device:TPU:0, one launch (start us, length us, event | category | flops | bytes accessed | tf_op | source)
XLA Modules:
  0.0 108.2 jit_solution(17519123632938801612)
XLA Ops:
  6.5 3.6 %copy.43 = bf16[128,8,16,128]{3,2,1,0:T(8,128)(2,1)S(1)} copy(bf16[128,8,16,128]{3,1,2,0:T(8,128)(2,1)} %bitcast.56) | data formatting | bytes 8388608
  10.2 3.1 %copy.30 = bf16[16,64,16,128]{3,1,2,0:T(8,128)(2,1)} copy(bf16[16,64,16,128]{3,2,1,0:T(8,128)(2,1)S(1)} %bitcast.54) | data formatting | bytes 8388608 | tf_op jit(solution)/shard_map/reshape | solution.py:16
  13.4 2.9 %gather_fusion.2 = bf16[4,16,64,128]{3,2,1,0:T(8,128)(2,1)S(1)} fusion(bf16[16,64,16,128]{3,1,2,0:T(8,128)(2,1)} %copy.30, s32[1024]{0:T(1024)S(1)} %pad_clamp_fusion), kind=kCustom, calls=%fused_computation.2.clone | custom fusion | bytes 2097168 | tf_op jit(solution)/shard_map/jit(_take)/gather | solution.py:17
  16.3 0.6 gather_fusion.3
  16.9 0.2 bitcast_multiply_fusion
  17.1 0.9 copy.32
  18.0 0.4 reshape.55
  18.6 3.6 %copy.42 = bf16[128,8,16,128]{3,2,1,0:T(8,128)(2,1)S(1)} copy(bf16[128,8,16,128]{3,1,2,0:T(8,128)(2,1)} %bitcast.57) | data formatting | bytes 8388608
  22.2 3.1 %copy.25 = bf16[16,64,16,128]{3,1,2,0:T(8,128)(2,1)} copy(bf16[16,64,16,128]{3,2,1,0:T(8,128)(2,1)S(1)} %bitcast.55) | data formatting | bytes 8388608 | tf_op jit(solution)/shard_map/reshape | solution.py:16
  25.3 2.9 %gather_fusion = bf16[4,16,64,128]{3,2,1,0:T(8,128)(2,1)S(1)} fusion(bf16[16,64,16,128]{3,1,2,0:T(8,128)(2,1)} %copy.25, s32[1024]{0:T(1024)S(1)} %pad_clamp_fusion.1), kind=kCustom, calls=%fused_computation.clone | custom fusion | bytes 2097168 | tf_op jit(solution)/shard_map/jit(_take)/gather | solution.py:17
  28.3 0.6 gather_fusion.1
  29.1 0.9 copy.27
  30.0 0.4 reshape.51
  30.6 0.4 fusion.1
  31.0 0.4 fusion.4
  31.4 0.8 pad_maximum_fusion
  32.4 24.4 %reduce-scatter.3.cloned.1.call-done = f32[256,128]{0,1:T(8,128)} async-done(((f32[1024,128]{0,1:T(8,128)}), f32[256,128]{0,1:T(8,128)}) %reduce-scatter.3.cloned.1.call-update) | async-done | bytes 131088 | tf_op jit(solution)/shard_map/reduce_scatter | solution.py:57
  56.8 0.9 fusion.15
  57.9 0.3 convolution_multiply_fusion
  58.3 6.5 %all_to_all.19 = f32[4,2,2048]{2,0,1:T(4,128)S(1)} all-to-all(f32[4,2,2048]{2,0,1:T(4,128)S(1)} %copy.37), channel_id=1, replica_groups=mesh['grp'=2,'seq'=4,'wid'=2,'rep'=2] {'wid'}, dimensions={1} | all-to-all | bytes 131072 | tf_op jit(solution)/shard_map/all_to_all | solution.py:68
  64.9 13.9 %all_gather.3 = f32[32,2048]{1,0:T(8,128)S(1)} all-gather(f32[8,2048]{1,0:T(8,128)S(1)} %all_to_all.17), channel_id=1, replica_groups=mesh['grp'=2,'seq'=4,'wid'=2,'rep'=2] {'seq'}, dimensions={0}, use_global_device_ids=true | all-gather | bytes 327680 | tf_op jit(solution)/shard_map/all_gather | solution.py:69
  78.7 10.6 %fusion.16 = f32[32,1024]{1,0:T(8,128)} fusion(f32[32,2048]{1,0:T(8,128)S(1)} %all_gather.3, f32[1024,2048]{1,0:T(8,128)} %param.21), kind=kOutput, calls=%fused_computation.38 | convolution fusion | flops 805306368 | bytes 8781824 | tf_op jit(solution)/shard_map/dot_general | solution.py:28
  89.3 10.5 %reduce-scatter.5.cloned.1.call-done = f32[16,1024]{1,0:T(8,128)} async-done(((f32[32,1024]{1,0:T(8,128)}), f32[16,1024]{1,0:T(8,128)}) %reduce-scatter.5.cloned.1.call-update) | async-done | bytes 65552 | tf_op jit(solution)/shard_map/reduce_scatter | solution.py:70
  99.8 1.5 %copy.38 = f32[16,1,1024]{2,1,0:T(1,128)} copy(f32[16,1,1024]{2,0,1:T(8,128)} %bitcast.64) | data formatting | bytes 131072 | tf_op jit(solution)/shard_map/reshape | solution.py:71
  (32 shorter events, 1.2 us)
Async XLA Ops:
  6.5 24.0 %copy-start = (bf16[4,128,64]{1,2,0:T(8,128)(2,1)S(1)}, bf16[4,128,64]{1,2,0:T(8,128)(2,1)}, u32[]{:S(2)}) copy-start(bf16[4,128,64]{1,2,0:T(8,128)(2,1)} %param.19) | copy-start | bytes 196612
  6.5 50.3 %reduce-scatter.3.cloned.1.call-start = ((), (), s32[]{:S(2)}) async-start(), calls=%async_computation.3 | async-start | bytes 655360 | tf_op jit(solution)/shard_map/reduce_scatter | solution.py:57
  10.2 3.1 %copy-start.4 = (s32[4]{0:T(128)S(1)}, s32[4]{0:T(128)}, u32[]{:S(2)}) copy-start(s32[4]{0:T(128)} %param.20) | copy-start | bytes 52
  10.2 3.1 %copy-start.2 = (s32[16,16]{1,0:T(8,128)S(1)}, s32[16,16]{1,0:T(8,128)}, u32[]{:S(2)}) copy-start(s32[16,16]{1,0:T(8,128)} %param.16) | copy-start | bytes 3076
  22.1 3.1 %copy-start.5 = (s32[4]{0:T(128)S(1)}, s32[4]{0:T(128)}, u32[]{:S(2)}) copy-start(s32[4]{0:T(128)} %param.18) | copy-start | bytes 52
  22.2 3.1 %copy-start.3 = (s32[16,16]{1,0:T(8,128)S(1)}, s32[16,16]{1,0:T(8,128)}, u32[]{:S(2)}) copy-start(s32[16,16]{1,0:T(8,128)} %param.15) | copy-start | bytes 3076
  29.1 1.9 %copy-start.1 = (bf16[4,128,64]{1,2,0:T(8,128)(2,1)S(1)}, bf16[4,128,64]{1,2,0:T(8,128)(2,1)}, u32[]{:S(2)}) copy-start(bf16[4,128,64]{1,2,0:T(8,128)(2,1)} %param.17) | copy-start | bytes 196612
  32.3 67.5 %reduce-scatter.5.cloned.1.call-start = ((), (), s32[]{:S(2)}) async-start(), calls=%async_computation.4 | async-start | bytes 196608 | tf_op jit(solution)/shard_map/reduce_scatter | solution.py:70
Sparse Core Ops, SparseCore 0:
  32.4 24.3 reduce-scatter.2
  89.5 10.3 reduce-scatter.4
where the time goes:
time: 109 us; the launch traced here: 108 us
  waiting for transfers between devices  34.9 us (32%)
  local copies, waits for them, and re-layouts  26.1 us (24%)
  blocking collectives  20.4 us (19%)
  between operations  13.6 us (12%)
  matrix products  11.7 us (11%)
  other arithmetic  1.38 us (1%)
    reduce_scatter x1, waiting for transfers between devices, shards(): lax.psum_scatter(jnp.concatenate([act_part, grad_part], axis=1), ('wid',...  24.4 us
    all_gather x1, blocking collectives, shards(): lax.all_gather(routed, 'seq', axis=0, tiled=True)  13.9 us
    dot_general x1, matrix products, tile_product(): lax.dot_general(piece_rows, fisher_tile, (((1,), (1,)), ((), ())), precis...  10.6 us
    reduce_scatter x1, waiting for transfers between devices, shards(): lax.psum_scatter(partial_value, 'wid', scatter_dimension=0, tiled=True)  10.5 us
    unnamed x16, local copies, waits for them, and re-layouts  7.37 us
    all_to_all x1, blocking collectives, shards(): lax.all_to_all(flat, 'wid', split_axis=1, concat_axis=0, tiled=True)  6.5 us
    reshape x2, local copies, waits for them, and re-layouts, select_blocks(): blocks = values.reshape(seq_local, LEN, block_count, BLK)  6.13 us
    gather x2, local copies, waits for them, and re-layouts, select_blocks(): picked = jnp.take(blocks, local_index, axis=2)  5.87 us
  transfers between devices with their start and end apart: 2, of which 2 were waited for; matrix products, arithmetic and copies ran while one was open for 0% of the time, Pallas kernels for 0%

commit v1 on v0

v1 whole, which is shorter than its diff:
```python
import functools

import jax
import jax.numpy as jnp
from jax import lax
from jax.experimental import pallas as pl
from jax.experimental.pallas import tpu as pltpu
from jax.sharding import PartitionSpec as P

BLK = 128
LEN = 64
MESH = pl.DeviceIdType.MESH
NT = (((1,), (1,)), ((), ()))


def split(value):
    high = value.astype(jnp.bfloat16)
    low = (value - high.astype(jnp.float32)).astype(jnp.bfloat16)
    return high, low


def project_kernel(
    rep_count,
    block_count,
    act_index,
    grad_index,
    act_exp,
    grad_exp,
    act_blocks,
    grad_blocks,
    acts,
    grads,
    out,
    held,
    sems,
):
    chosen = act_blocks.shape[0]
    width = act_blocks.shape[1]
    seqs = act_exp.shape[0]
    per_rep = seqs // rep_count
    sides = ((grad_index, grad_exp, grad_blocks, grads), (act_index, act_exp, act_blocks, acts))
    copies = []
    for side, (index, _, _, values) in enumerate(sides):
        for b in range(chosen):
            at = pl.multiple_of(lax.rem(index[b], block_count) * BLK, BLK)
            copy = pltpu.make_async_copy(
                values.at[:, pl.ds(at, BLK)], held.at[side, b], sems.at[side, b]
            )
            copy.start()
            copies.append(copy)
    for side, (index, exps, blocks, _) in enumerate(sides):
        scaled = [[] for _ in range(rep_count)]
        for b in range(chosen):
            copies[side * chosen + b].wait()
            local = lax.rem(index[b], block_count)
            for k in range(rep_count):
                rows = []
                for l in range(per_rep):
                    s = l * rep_count + k
                    power = jnp.exp2(jnp.full((LEN, BLK), exps[s, local], jnp.int32).astype(jnp.float32))
                    rows.append(held[side, b, pl.ds(s * LEN, LEN), :] * power.astype(jnp.bfloat16))
                scaled[k].append(jnp.concatenate(rows, axis=0))
        weight = jnp.concatenate([blocks[b] for b in range(chosen)], axis=1)
        for k in range(rep_count):
            out[k, pl.ds(side * width, width), :] = lax.dot_general(
                weight, jnp.concatenate(scaled[k], axis=1), NT, preferred_element_type=jnp.float32
            )


def main_kernel(
    counts,
    proj,
    fisher,
    out,
    rep_in,
    summed,
    wid_in,
    outers,
    fisher_f32,
    fisher_high,
    fisher_low,
    partial_value,
    result_in,
    fisher_sems,
    rep_sems,
    wid_sems,
    seq_sems,
    result_sems,
):
    seq_count, wid_count, rep_count = counts
    q = lax.axis_index("seq")
    w = lax.axis_index("wid")
    r = lax.axis_index("rep")
    width = proj.shape[1] // 2
    tokens = proj.shape[2]
    slice_rows = width // wid_count
    pairs = slice_rows // 2
    per_rep = tokens // LEN
    fisher_rows = fisher.shape[0]
    parts = fisher_sems.shape[0]
    part_rows = fisher_rows // parts

    fisher_copies = []
    for f in range(parts):
        rows = pl.ds(f * part_rows, part_rows)
        copy = pltpu.make_async_copy(fisher.at[rows, :], fisher_f32.at[rows, :], fisher_sems.at[f])
        copy.start()
        fisher_copies.append(copy)

    peers = (
        [{"rep": lax.rem(r + d, rep_count)} for d in range(1, rep_count)]
        + [{"wid": lax.rem(w + d, wid_count)} for d in range(1, wid_count)]
        + [{"seq": lax.rem(q + d, seq_count)} for d in range(1, seq_count)]
    )
    barrier = pltpu.get_barrier_semaphore()
    for peer in peers:
        pl.semaphore_signal(barrier, inc=1, device_id=peer, device_id_type=MESH)
    pl.semaphore_wait(barrier, len(peers))

    def send(src, dst, sems, slot, peer):
        copy = pltpu.make_async_remote_copy(
            src_ref=src,
            dst_ref=dst,
            send_sem=sems.at[0, slot],
            recv_sem=sems.at[1, slot],
            device_id=peer,
            device_id_type=MESH,
        )
        copy.start()
        return copy

    rep_copies = []
    for d in range(1, rep_count):
        to = lax.rem(r + d, rep_count)
        rep_copies.append(send(proj.at[to], rep_in.at[d - 1], rep_sems, d - 1, {"rep": to}))
    for copy in rep_copies:
        copy.wait_recv()
    total = proj[r]
    for d in range(1, rep_count):
        total = total + rep_in[d - 1]
    summed[...] = total

    wid_copies = []
    for d in range(1, wid_count):
        to = lax.rem(w + d, wid_count)
        wid_copies.append(
            send(
                summed.at[pl.ds(width, width), :],
                wid_in.at[d - 1, pl.ds(0, width), :],
                wid_sems,
                2 * d - 2,
                {"wid": to},
            )
        )
        wid_copies.append(
            send(
                summed.at[pl.ds(pl.multiple_of(to * slice_rows, 8), slice_rows), :],
                wid_in.at[d - 1, pl.ds(width, slice_rows), :],
                wid_sems,
                2 * d - 1,
                {"wid": to},
            )
        )

    for f in range(parts):
        fisher_copies[f].wait()

        @pl.loop(0, part_rows // 32)
        def _(step):
            rows = pl.ds(pl.multiple_of(f * part_rows + step * 32, 32), 32)
            high, low = split(fisher_f32[rows, :])
            fisher_high[rows, :] = high
            fisher_low[rows, :] = low

    for copy in wid_copies:
        copy.wait_recv()
    act = summed[pl.ds(width, width), :]
    grad = summed[pl.ds(pl.multiple_of(w * slice_rows, 8), slice_rows), :]
    for d in range(1, wid_count):
        act = act + wid_in[d - 1, pl.ds(0, width), :]
        grad = grad + wid_in[d - 1, pl.ds(width, slice_rows), :]
    act_high, act_low = split(act)
    grad = grad * (1.0 / LEN)
    grad_high = grad.astype(jnp.bfloat16).astype(jnp.float32)
    grad_low = grad - grad_high
    own = lax.broadcasted_iota(jnp.int32, (per_rep, tokens), 1) // LEN == lax.broadcasted_iota(
        jnp.int32, (per_rep, tokens), 0
    )

    def spread(rows_of, first):
        rows = []
        for i in range(first, slice_rows, 2):
            row = jnp.broadcast_to(rows_of[i : i + 1, :], (per_rep, tokens))
            rows.append(jnp.where(own, row, 0.0))
        return jnp.concatenate(rows, axis=0).astype(jnp.bfloat16)

    halves = []
    for first in range(2):
        high = spread(grad_high, first)
        low = spread(grad_low, first)
        halves.append(
            lax.dot_general(high, act_high, NT, preferred_element_type=jnp.float32)
            + (
                lax.dot_general(low, act_high, NT, preferred_element_type=jnp.float32)
                + lax.dot_general(high, act_low, NT, preferred_element_type=jnp.float32)
            )
        )
    outers[q] = jnp.concatenate(halves, axis=1).reshape(pairs, per_rep, 2 * width)

    seq_copies = []
    for d in range(1, seq_count):
        to = lax.rem(q + d, seq_count)
        seq_copies.append(send(outers.at[q], outers.at[q], seq_sems, d - 1, {"seq": to}))
    for copy in seq_copies:
        copy.wait_recv()

    rows = seq_count * per_rep
    flat = jnp.concatenate([outers[:, p].reshape(rows, 2 * width) for p in range(pairs)], axis=1)
    flat_high, flat_low = split(flat)
    both = jnp.concatenate([flat_high, flat_low], axis=0)
    own_rows = rows // wid_count
    tile = min(fisher_rows, 256)
    for t in range(fisher_rows // tile):
        at = pl.ds(t * tile, tile)
        first = lax.dot_general(fisher_high[at, :], both, NT, preferred_element_type=jnp.float32)
        second = lax.dot_general(fisher_low[at, :], flat_high, NT, preferred_element_type=jnp.float32)
        first = first.T
        value = first[:rows, :] + (first[rows:, :] + second.T)
        partial_value[:, :, at] = value.reshape(wid_count, own_rows, tile)

    result_copies = []
    for d in range(1, wid_count):
        to = lax.rem(w + d, wid_count)
        result_copies.append(
            send(partial_value.at[to], result_in.at[d - 1], result_sems, d - 1, {"wid": to})
        )
    for copy in result_copies:
        copy.wait_recv()
    value = partial_value[w]
    for d in range(1, wid_count):
        value = value + result_in[d - 1]
    out[...] = value.reshape(own_rows, 1, fisher_rows)
    for copy in rep_copies + wid_copies + seq_copies + result_copies:
        copy.wait_send()


def shards(
    activations,
    output_grads,
    act_exponents,
    grad_exponents,
    input_blocks,
    input_index,
    output_blocks,
    output_index,
    fisher_inverse,
):
    seq_count = lax.axis_size("seq")
    wid_count = lax.axis_size("wid")
    rep_count = lax.axis_size("rep")
    chosen, _, width = input_blocks.shape
    tok_rows = activations.shape[0]
    block_count = activations.shape[1] // BLK
    tokens = tok_rows // rep_count
    per_rep = tokens // LEN
    slice_rows = width // wid_count
    rows = seq_count * per_rep
    own_rows = rows // wid_count
    fisher_rows, fisher_cols = fisher_inverse.shape
    vmem = pl.BlockSpec(memory_space=pltpu.VMEM)
    smem = pl.BlockSpec(memory_space=pltpu.SMEM)
    hbm = pl.BlockSpec(memory_space=pltpu.HBM)
    f32 = jnp.float32
    dma = pltpu.SemaphoreType.DMA
    projected = pl.pallas_call(
        functools.partial(project_kernel, rep_count, block_count),
        out_shape=jax.ShapeDtypeStruct((rep_count, 2 * width, tokens), f32),
        in_specs=[smem, smem, smem, smem, vmem, vmem, hbm, hbm],
        out_specs=vmem,
        scratch_shapes=[pltpu.VMEM((2, chosen, tok_rows, BLK), jnp.bfloat16), dma((2, chosen))],
        compiler_params=pltpu.CompilerParams(vmem_limit_bytes=56 << 20),
        name="project",
    )(
        input_index,
        output_index,
        act_exponents,
        grad_exponents,
        jnp.swapaxes(input_blocks, 1, 2),
        jnp.swapaxes(output_blocks, 1, 2),
        activations,
        output_grads,
    )
    return pl.pallas_call(
        functools.partial(main_kernel, (seq_count, wid_count, rep_count)),
        out_shape=jax.ShapeDtypeStruct((own_rows, 1, fisher_rows), f32),
        in_specs=[vmem, hbm],
        out_specs=vmem,
        scratch_shapes=[
            pltpu.VMEM((rep_count - 1, 2 * width, tokens), f32),
            pltpu.VMEM((2 * width, tokens), f32),
            pltpu.VMEM((wid_count - 1, width + slice_rows, tokens), f32),
            pltpu.VMEM((seq_count, slice_rows // 2, per_rep, 2 * width), f32),
            pltpu.VMEM((fisher_rows, fisher_cols), f32),
            pltpu.VMEM((fisher_rows, fisher_cols), jnp.bfloat16),
            pltpu.VMEM((fisher_rows, fisher_cols), jnp.bfloat16),
            pltpu.VMEM((wid_count, own_rows, fisher_rows), f32),
            pltpu.VMEM((wid_count - 1, own_rows, fisher_rows), f32),
            dma((4,)),
            dma((2, rep_count - 1)),
            dma((2, 2 * (wid_count - 1))),
            dma((2, seq_count - 1)),
            dma((2, wid_count - 1)),
        ],
        compiler_params=pltpu.CompilerParams(
            collective_id=0, has_side_effects=True, vmem_limit_bytes=56 << 20
        ),
        name="exchange",
    )(projected, fisher_inverse)


def solution(mesh):
    placed = (
        P(("grp", "seq"), ("wid", "rep")),
        P(("grp", "seq"), ("wid", "rep")),
        P(("grp", "seq"), ("wid", "rep")),
        P(("grp", "seq"), ("wid", "rep")),
        P(("wid", "rep"), None, None),
        P(("wid", "rep")),
        P(("wid", "rep"), None, None),
        P(("wid", "rep")),
        P("seq", "wid"),
    )
    return jax.shard_map(
        shards,
        mesh=mesh,
        in_specs=placed,
        out_specs=P(("grp", "wid"), "rep", "seq"),
        check_vma=False,
    )
```

time: 109 us -> 32.2 us (0.30)
  waiting for transfers between devices: 34.9 us -> 0 us
  Pallas kernels: 0 us -> 30.4 us
  local copies, waits for them, and re-layouts: 26.1 us -> 1.47 us
  blocking collectives: 20.4 us -> 0 us
  between operations: 13.6 us -> 0.02 us
  matrix products: 11.7 us -> 0 us
  other arithmetic: 1.38 us -> 0 us
    reduce_scatter x2 -> x0, waiting for transfers between devices: 34.9 us -> none  [the longest x1 24.4 us: shards(): lax.psum_scatter(jnp.concatenate([act_part, grad_part], axis=1), ('wid',...]
    pallas_call x0 -> x2, Pallas kernels: none -> 30.4 us  [the longest x1 26.3 us: shards(): pl.pallas_call(functools.partial(main_kernel, (seq_count, wid_count, rep_...]
    all_gather x1 -> x0, blocking collectives: 13.9 us -> none  [shards(): lax.all_gather(routed, 'seq', axis=0, tiled=True)]
    dot_general x4 -> x0, matrix products: 11.7 us -> none  [the longest x1 10.6 us: tile_product(): lax.dot_general(piece_rows, fisher_tile, (((1,), (1,)), ((), ())), precis...]
    reshape x7 -> x0, local copies, waits for them, and re-layouts: 8.75 us -> none  [the longest x2 6.13 us: select_blocks(): blocks = values.reshape(seq_local, LEN, block_count, BLK)]
    gather x4 -> x0, local copies, waits for them, and re-layouts: 6.99 us -> none  [the longest x2 5.87 us: select_blocks(): picked = jnp.take(blocks, local_index, axis=2)]
    all_to_all x1 -> x0, blocking collectives: 6.5 us -> none  [shards(): lax.all_to_all(flat, 'wid', split_axis=1, concat_axis=0, tiled=True)]
    unnamed x16 -> x1, local copies, waits for them, and re-layouts: 7.37 us -> 1.47 us
  transfers between devices with their start and end apart: 2 -> 0, of which waited for: 2 -> 0; matrix products, arithmetic and copies ran while one was open for 0% -> 0% of each run, Pallas kernels for 0% -> 0%
where the time goes in v1:
time: 32.2 us; the launch traced here: 31.9 us
  Pallas kernels  30.4 us (94%)
  local copies, waits for them, and re-layouts  1.47 us (5%)
    pallas_call x1, Pallas kernels, shards(): pl.pallas_call(functools.partial(main_kernel, (seq_count, wid_count, rep_...  26.3 us
    pallas_call x1, Pallas kernels, shards(): pl.pallas_call(functools.partial(project_kernel, rep_count, block_count),...  4.08 us
    unnamed x1, local copies, waits for them, and re-layouts  1.47 us

profile of v1, /device:TPU:0, one launch (start us, length us, event | category | flops | bytes accessed | tf_op | source)
XLA Modules:
  0.0 31.9 jit_solution(12154664681237316279)
XLA Ops:
  0.0 4.1 %project.1.proj = f32[2,128,512]{2,1,0:T(8,128)} custom-call(s32[4]{0:T(128)} %act_index.1, s32[4]{0:T(128)} %grad_index.1, s32[16,16]{1,0:T(8,128)} %act_exp.1, s32[16,16]{1,0:T(8,128)} %grad_exp.1, bf16[4,64,128]{2,1,0:T(8,128)(2,1)} %bitcast.2, bf16[4,64,128]{2,1,0:T(8,128)(2,1)} %bitcast.3, bf16[1024,2048]{1,0:T(8,128)(2,1)} %acts.1, ...), custom_call_target="tpu_custom_call" | custom-call | tf_op jit(solution)/shard_map/project/pallas_call | solution.py:275
  4.1 26.3 %exchange.1 = f32[16,1,1024]{2,1,0:T(1,128)} custom-call(f32[2,128,512]{2,1,0:T(8,128)} %project.1.proj, f32[1024,2048]{1,0:T(8,128)} %fisher.1), custom_call_target="tpu_custom_call" | custom-call | tf_op jit(solution)/shard_map/exchange/pallas_call | solution.py:293
  30.4 1.5 %copy.11 = f32[16,1,1024]{2,1,0:T(1,128)} copy(f32[16,1,1024]{2,1,0:T(1,128)} %exchange.1) | data formatting | bytes 131072

commit v2 on v0

v2 whole, which is shorter than its diff:
```python
import functools

import jax
import jax.numpy as jnp
from jax import lax
from jax.experimental import pallas as pl
from jax.experimental.pallas import tpu as pltpu
from jax.sharding import PartitionSpec as P

BLK = 128
LEN = 64
MESH = pl.DeviceIdType.MESH
NT = (((1,), (1,)), ((), ()))


def split(value):
    high = value.astype(jnp.bfloat16)
    low = (value - high.astype(jnp.float32)).astype(jnp.bfloat16)
    return high, low


def kernel(
    counts,
    chunks,
    act_index,
    grad_index,
    act_exp,
    grad_exp,
    act_blocks,
    grad_blocks,
    acts,
    grads,
    fisher,
    out,
    held,
    proj,
    rep_in,
    summed,
    wid_in,
    outers,
    flat,
    fisher_f32,
    fisher_high,
    fisher_low,
    partial_value,
    result_in,
    held_sems,
    fisher_sems,
    rep_sems,
    wid_sems,
    seq_sems,
    result_sems,
):
    seq_count, wid_count, rep_count = counts
    q = lax.axis_index("seq")
    w = lax.axis_index("wid")
    r = lax.axis_index("rep")
    chosen, width, _ = act_blocks.shape
    block_count = acts.shape[1] // BLK
    seqs = act_exp.shape[0]
    per_rep = seqs // rep_count
    chunk_seqs = per_rep // chunks
    tokens = chunk_seqs * LEN
    slice_rows = width // wid_count
    pairs = slice_rows // 2
    fisher_rows = fisher.shape[0]
    parts = fisher_sems.shape[0]
    part_rows = fisher_rows // parts
    rows = seq_count * per_rep
    own_rows = rows // wid_count
    tiles, _, _, tile = partial_value.shape

    peers = (
        [{"rep": lax.rem(r + d, rep_count)} for d in range(1, rep_count)]
        + [{"wid": lax.rem(w + d, wid_count)} for d in range(1, wid_count)]
        + [{"seq": lax.rem(q + d, seq_count)} for d in range(1, seq_count)]
    )
    barrier = pltpu.get_barrier_semaphore()
    for peer in peers:
        pl.semaphore_signal(barrier, inc=1, device_id=peer, device_id_type=MESH)

    sides = ((grad_index, grad_exp, grad_blocks, grads), (act_index, act_exp, act_blocks, acts))
    held_copies = []
    for c in range(chunks):
        span = pl.ds(c * rep_count * tokens, rep_count * tokens)
        for side in range(2):
            for b in range(block_count):
                copy = pltpu.make_async_copy(
                    sides[side][3].at[span, pl.ds(b * BLK, BLK)],
                    held[2 * c + side].at[b],
                    held_sems.at[c, side, b],
                )
                copy.start()
                held_copies.append(copy)
    fisher_copies = []
    for f in range(parts):
        span = pl.ds(f * part_rows, part_rows)
        copy = pltpu.make_async_copy(fisher.at[span, :], fisher_f32.at[span, :], fisher_sems.at[f])
        copy.start()
        fisher_copies.append(copy)

    def send(src, dst, sems, slot, peer):
        copy = pltpu.make_async_remote_copy(
            src_ref=src,
            dst_ref=dst,
            send_sem=sems.at[(0, *slot)],
            recv_sem=sems.at[(1, *slot)],
            device_id=peer,
            device_id_type=MESH,
        )
        copy.start()
        return copy

    def project(c):
        for side, (index, exps, blocks, _) in enumerate(sides):
            for b in range(block_count):
                held_copies[(2 * c + side) * block_count + b].wait()
            scaled = [[] for _ in range(rep_count)]
            for b in range(chosen):
                local = lax.rem(index[b], block_count)
                for k in range(rep_count):
                    pieces = []
                    for l in range(chunk_seqs):
                        s = l * rep_count + k
                        exponent = exps[c * chunk_seqs * rep_count + s, local]
                        power = jnp.exp2(jnp.full((LEN, BLK), exponent, jnp.int32).astype(jnp.float32))
                        values = held[2 * c + side][local, pl.ds(s * LEN, LEN), :]
                        pieces.append(values * power.astype(jnp.bfloat16))
                    scaled[k].append(jnp.concatenate(pieces, axis=0))
            weight = jnp.concatenate([blocks[b] for b in range(chosen)], axis=1)
            for k in range(rep_count):
                proj[c, k, pl.ds(side * width, width), :] = lax.dot_general(
                    weight,
                    jnp.concatenate(scaled[k], axis=1),
                    NT,
                    preferred_element_type=jnp.float32,
                )

    def split_fisher(f):
        fisher_copies[f].wait()

        @pl.loop(0, part_rows // 32)
        def _(step):
            span = pl.ds(pl.multiple_of(f * part_rows + step * 32, 32), 32)
            high, low = split(fisher_f32[span, :])
            fisher_high[span, :] = high
            fisher_low[span, :] = low

    rep_copies = [[] for _ in range(chunks)]
    for c in range(chunks):
        project(c)
        if c == 0:
            pl.semaphore_wait(barrier, len(peers))
        for d in range(1, rep_count):
            to = lax.rem(r + d, rep_count)
            rep_copies[c].append(
                send(proj.at[c, to], rep_in.at[d - 1, c], rep_sems, (d - 1, c), {"rep": to})
            )

    wid_copies = [[] for _ in range(chunks)]
    for c in range(chunks):
        for copy in rep_copies[c]:
            copy.wait_recv()
        total = proj[c, r]
        for d in range(1, rep_count):
            total = total + rep_in[d - 1, c]
        summed[c] = total
        for d in range(1, wid_count):
            to = lax.rem(w + d, wid_count)
            wid_copies[c].append(
                send(
                    summed.at[c, pl.ds(width, width), :],
                    wid_in.at[d - 1, c, pl.ds(0, width), :],
                    wid_sems,
                    (2 * d - 2, c),
                    {"wid": to},
                )
            )
            wid_copies[c].append(
                send(
                    summed.at[c, pl.ds(pl.multiple_of(to * slice_rows, 8), slice_rows), :],
                    wid_in.at[d - 1, c, pl.ds(width, slice_rows), :],
                    wid_sems,
                    (2 * d - 1, c),
                    {"wid": to},
                )
            )

    for f in range(parts // 2):
        split_fisher(f)

    row = lax.broadcasted_iota(jnp.int32, (8, tokens), 0)
    own = lax.broadcasted_iota(jnp.int32, (8, tokens), 1) // LEN == row % chunk_seqs
    group = 8 // chunk_seqs

    def spread(rows_of, first):
        pieces = []
        for p in range(0, pairs, group):
            value = jnp.broadcast_to(rows_of[2 * p + first : 2 * p + first + 1, :], (8, tokens))
            for j in range(1, group):
                i = 2 * (p + j) + first
                value = jnp.where(
                    row // chunk_seqs == j, jnp.broadcast_to(rows_of[i : i + 1, :], (8, tokens)), value
                )
            pieces.append(jnp.where(own, value, 0.0))
        return jnp.concatenate(pieces, axis=0).astype(jnp.bfloat16)

    seq_copies = [[] for _ in range(chunks)]
    for c in range(chunks):
        for copy in wid_copies[c]:
            copy.wait_recv()
        act = summed[c, pl.ds(width, width), :]
        grad = summed[c, pl.ds(pl.multiple_of(w * slice_rows, 8), slice_rows), :]
        for d in range(1, wid_count):
            act = act + wid_in[d - 1, c, pl.ds(0, width), :]
            grad = grad + wid_in[d - 1, c, pl.ds(width, slice_rows), :]
        act_high, act_low = split(act)
        grad = grad * (1.0 / LEN)
        grad_high = grad.astype(jnp.bfloat16).astype(jnp.float32)
        grad_low = grad - grad_high
        halves = []
        for first in range(2):
            high = spread(grad_high, first)
            low = spread(grad_low, first)
            halves.append(
                lax.dot_general(high, act_high, NT, preferred_element_type=jnp.float32)
                + (
                    lax.dot_general(low, act_high, NT, preferred_element_type=jnp.float32)
                    + lax.dot_general(high, act_low, NT, preferred_element_type=jnp.float32)
                )
            )
        outers[q, c] = jnp.concatenate(halves, axis=1)
        for d in range(1, seq_count):
            to = lax.rem(q + d, seq_count)
            seq_copies[c].append(
                send(outers.at[q, c], outers.at[q, c], seq_sems, (d - 1, c), {"seq": to})
            )

    for f in range(parts // 2, parts):
        split_fisher(f)

    for c in range(chunks):
        for copy in seq_copies[c]:
            copy.wait_recv()
        for o in range(seq_count):
            for p in range(pairs):
                flat[pl.ds(o * per_rep + c * chunk_seqs, chunk_seqs), pl.ds(p * BLK, BLK)] = outers[
                    o, c, pl.ds(p * chunk_seqs, chunk_seqs), :
                ]

    flat_high, flat_low = split(flat[...])
    both = jnp.concatenate([flat_high, flat_low], axis=0)
    result_copies = []
    for t in range(tiles):
        at = pl.ds(t * tile, tile)
        first = lax.dot_general(fisher_high[at, :], both, NT, preferred_element_type=jnp.float32)
        second = lax.dot_general(fisher_low[at, :], flat_high, NT, preferred_element_type=jnp.float32)
        first = first.T
        value = first[:rows, :] + (first[rows:, :] + second.T)
        partial_value[t] = value.reshape(wid_count, own_rows, tile)
        for d in range(1, wid_count):
            to = lax.rem(w + d, wid_count)
            result_copies.append(
                send(
                    partial_value.at[t, to],
                    result_in.at[d - 1, t],
                    result_sems,
                    (d - 1, t),
                    {"wid": to},
                )
            )
    for copy in result_copies:
        copy.wait_recv()
    for t in range(tiles):
        value = partial_value[t, w]
        for d in range(1, wid_count):
            value = value + result_in[d - 1, t]
        out[:, :, pl.ds(t * tile, tile)] = value.reshape(own_rows, 1, tile)
    for copies in rep_copies + wid_copies + seq_copies + [result_copies]:
        for copy in copies:
            copy.wait_send()


def shards(
    activations,
    output_grads,
    act_exponents,
    grad_exponents,
    input_blocks,
    input_index,
    output_blocks,
    output_index,
    fisher_inverse,
):
    seq_count = lax.axis_size("seq")
    wid_count = lax.axis_size("wid")
    rep_count = lax.axis_size("rep")
    chunks = 2
    width = input_blocks.shape[2]
    tok_rows, features = activations.shape
    per_rep = tok_rows // LEN // rep_count
    tokens = per_rep // chunks * LEN
    slice_rows = width // wid_count
    pairs = slice_rows // 2
    rows = seq_count * per_rep
    own_rows = rows // wid_count
    fisher_rows, fisher_cols = fisher_inverse.shape
    tile = min(fisher_rows, 256)
    tiles = fisher_rows // tile
    parts = 4
    vmem = pl.BlockSpec(memory_space=pltpu.VMEM)
    smem = pl.BlockSpec(memory_space=pltpu.SMEM)
    hbm = pl.BlockSpec(memory_space=pltpu.HBM)
    f32 = jnp.float32
    dma = pltpu.SemaphoreType.DMA
    return pl.pallas_call(
        functools.partial(kernel, (seq_count, wid_count, rep_count), chunks),
        out_shape=jax.ShapeDtypeStruct((own_rows, 1, fisher_rows), f32),
        in_specs=[smem, smem, smem, smem, vmem, vmem, hbm, hbm, hbm],
        out_specs=vmem,
        scratch_shapes=[
            [pltpu.VMEM((features // BLK, tok_rows // chunks, BLK), jnp.bfloat16)] * (2 * chunks),
            pltpu.VMEM((chunks, rep_count, 2 * width, tokens), f32),
            pltpu.VMEM((rep_count - 1, chunks, 2 * width, tokens), f32),
            pltpu.VMEM((chunks, 2 * width, tokens), f32),
            pltpu.VMEM((wid_count - 1, chunks, width + slice_rows, tokens), f32),
            pltpu.VMEM((seq_count, chunks, pairs * per_rep // chunks, 2 * width), f32),
            pltpu.VMEM((rows, pairs * 2 * width), f32),
            pltpu.VMEM((fisher_rows, fisher_cols), f32),
            pltpu.VMEM((fisher_rows, fisher_cols), jnp.bfloat16),
            pltpu.VMEM((fisher_rows, fisher_cols), jnp.bfloat16),
            pltpu.VMEM((tiles, wid_count, own_rows, tile), f32),
            pltpu.VMEM((wid_count - 1, tiles, own_rows, tile), f32),
            dma((chunks, 2, features // BLK)),
            dma((parts,)),
            dma((2, rep_count - 1, chunks)),
            dma((2, 2 * (wid_count - 1), chunks)),
            dma((2, seq_count - 1, chunks)),
            dma((2, wid_count - 1, tiles)),
        ],
        compiler_params=pltpu.CompilerParams(
            collective_id=0, has_side_effects=True, vmem_limit_bytes=56 << 20
        ),
        name="exchange",
    )(
        input_index,
        output_index,
        act_exponents,
        grad_exponents,
        jnp.swapaxes(input_blocks, 1, 2),
        jnp.swapaxes(output_blocks, 1, 2),
        activations,
        output_grads,
        fisher_inverse,
    )


def solution(mesh):
    placed = (
        P(("grp", "seq"), ("wid", "rep")),
        P(("grp", "seq"), ("wid", "rep")),
        P(("grp", "seq"), ("wid", "rep")),
        P(("grp", "seq"), ("wid", "rep")),
        P(("wid", "rep"), None, None),
        P(("wid", "rep")),
        P(("wid", "rep"), None, None),
        P(("wid", "rep")),
        P("seq", "wid"),
    )
    return jax.shard_map(
        shards,
        mesh=mesh,
        in_specs=placed,
        out_specs=P(("grp", "wid"), "rep", "seq"),
        check_vma=False,
    )
```

time: 109 us -> 29.6 us (0.27)
  waiting for transfers between devices: 34.9 us -> 0 us
  Pallas kernels: 0 us -> 28 us
  local copies, waits for them, and re-layouts: 26.1 us -> 1.47 us
  blocking collectives: 20.4 us -> 0 us
  between operations: 13.6 us -> 0.01 us
  matrix products: 11.7 us -> 0 us
  other arithmetic: 1.38 us -> 0 us
    reduce_scatter x2 -> x0, waiting for transfers between devices: 34.9 us -> none  [the longest x1 24.4 us: shards(): lax.psum_scatter(jnp.concatenate([act_part, grad_part], axis=1), ('wid',...]
    pallas_call x0 -> x1, Pallas kernels: none -> 28 us  [shards(): pl.pallas_call(functools.partial(kernel, (seq_count, wid_count, rep_count...]
    all_gather x1 -> x0, blocking collectives: 13.9 us -> none  [shards(): lax.all_gather(routed, 'seq', axis=0, tiled=True)]
    dot_general x4 -> x0, matrix products: 11.7 us -> none  [the longest x1 10.6 us: tile_product(): lax.dot_general(piece_rows, fisher_tile, (((1,), (1,)), ((), ())), precis...]
    reshape x7 -> x0, local copies, waits for them, and re-layouts: 8.75 us -> none  [the longest x2 6.13 us: select_blocks(): blocks = values.reshape(seq_local, LEN, block_count, BLK)]
    gather x4 -> x0, local copies, waits for them, and re-layouts: 6.99 us -> none  [the longest x2 5.87 us: select_blocks(): picked = jnp.take(blocks, local_index, axis=2)]
    all_to_all x1 -> x0, blocking collectives: 6.5 us -> none  [shards(): lax.all_to_all(flat, 'wid', split_axis=1, concat_axis=0, tiled=True)]
    unnamed x16 -> x1, local copies, waits for them, and re-layouts: 7.37 us -> 1.47 us
  transfers between devices with their start and end apart: 2 -> 0, of which waited for: 2 -> 0; matrix products, arithmetic and copies ran while one was open for 0% -> 0% of each run, Pallas kernels for 0% -> 0%
where the time goes in v2:
time: 29.6 us; the launch traced here: 29.4 us
  Pallas kernels  28 us (95%)
  local copies, waits for them, and re-layouts  1.47 us (5%)
    pallas_call x1, Pallas kernels, shards(): pl.pallas_call(functools.partial(kernel, (seq_count, wid_count, rep_count...  28 us
    unnamed x1, local copies, waits for them, and re-layouts  1.47 us

profile of v2, /device:TPU:0, one launch (start us, length us, event | category | flops | bytes accessed | tf_op | source)
XLA Modules:
  0.0 29.4 jit_solution(3042541199600595157)
XLA Ops:
  0.0 28.0 %exchange.1 = f32[16,1,1024]{2,1,0:T(1,128)} custom-call(s32[4]{0:T(128)} %act_index.1, s32[4]{0:T(128)} %grad_index.1, s32[16,16]{1,0:T(8,128)} %act_exp.1, s32[16,16]{1,0:T(8,128)} %grad_exp.1, bf16[4,64,128]{2,1,0:T(8,128)(2,1)} %bitcast.2, bf16[4,64,128]{2,1,0:T(8,128)(2,1)} %bitcast.3, bf16[1024,2048]{1,0:T(8,128)(2,1)} %acts.1, ...), custom_call_target="tpu_custom_call" | custom-call | tf_op jit(solution)/shard_map/exchange/pallas_call | solution.py:316
  28.0 1.5 %copy.11 = f32[16,1,1024]{2,1,0:T(1,128)} copy(f32[16,1,1024]{2,1,0:T(1,128)} %exchange.1) | data formatting | bytes 131072
